TPU v7x, 32 devices: a whole 2x2x4 slice. The times are simulated.
32 devices in a mesh: group: 4 (over x, core), dev: 8 (over z, y).
Axes of the slice: x: 2, y: 2, z: 4, core: 2. Of those that a mesh axis runs over, the one named last changes fastest.
Arguments:
- features: bfloat16 [131072, 128], P(('group', 'dev')), may hold values from -6 to 6
- coords: bfloat16 [3, 131072], P(None, ('group', 'dev')), may hold values from 0 to 1
- near_pairs: int32 [2, 256], P(None, 'group'), may hold values from 0 to 127, as said below
- parent_two: int32 [512], P(('group', 'dev')), may hold values from 0 to 31, as said below
- parent_three: int32 [128], P('group'), may hold values from 0 to 7
- rates: float32 [4], replicated, may hold values from 6 to 40
- w_near: bfloat16 [128, 128], replicated, may hold values from -0.5 to 0.5
- restrict: bfloat16 [64, 256], replicated, may hold values from -0.375 to 0.375
- w_two: bfloat16 [128, 128], replicated, may hold values from -0.5 to 0.5
- w_three: bfloat16 [128, 128], replicated, may hold values from -0.5 to 0.5
- w_four: bfloat16 [128, 128], replicated, may hold values from -0.5 to 0.5
- coupling: bfloat16 [32, 32], replicated, may hold values from -1 to 1
- expand: bfloat16 [256, 64], replicated, may hold values from -0.75 to 0.75
- w_out: bfloat16 [128, 128], replicated, may hold values from -0.5 to 0.5
Outputs:
- mixed: bfloat16 [131072, 128], P(('group', 'dev'))
Inputs may be any that keep to these rules, and one draw needn't show every extreme that they name: `near_pairs`: for any two devices A and P of dev in one region, at most 2 near pairs of that region have their first block on A and their second on P, and in each region some such two devices have exactly 2. `parent_two`: every level-two node of a region is named by exactly four blocks of that region.
All inputs are finite; a program needn't handle non-finite values.
Results may differ from a plain program's by a relative error of at most 0.008.
Values may be sent and summed in bfloat16 or wider, within the bound.
A program may use at most 128 MiB of HBM per device.

v0:
```python
import jax
import jax.numpy as jnp
from jax import lax
from jax.sharding import PartitionSpec as P

CAP = 2
NODES3_GROUP = 8


def kernel_table(cloud_one, cloud_two, rates):
    first_pos = cloud_one.astype(jnp.float32)
    second_pos = cloud_two.astype(jnp.float32)
    delta_x = first_pos[:, 0, :, None] - second_pos[:, 0, None, :]
    delta_y = first_pos[:, 1, :, None] - second_pos[:, 1, None, :]
    delta_z = first_pos[:, 2, :, None] - second_pos[:, 2, None, :]
    distance = delta_x * delta_x + delta_y * delta_y + delta_z * delta_z
    return jnp.exp(-rates[None, :, None, None] * distance[:, None]).astype(jnp.bfloat16)


def apply_table(kernel, block_values, head_count, transposed):
    channels = block_values.shape[-1]
    head_of = jnp.arange(channels, dtype=jnp.int32) // (channels // head_count)
    head_mask = (head_of[None, :] == jnp.arange(head_count, dtype=jnp.int32)[:, None]).astype(
        jnp.bfloat16
    )
    masked = block_values[:, None, :, :] * head_mask[None, :, None, :]
    form = "nhqp,nhqc->npc" if transposed else "nhpq,nhqc->npc"
    return jnp.einsum(form, kernel, masked, preferred_element_type=jnp.float32)


def in_groups(array):
    return array.reshape((array.shape[0] // 8, 8) + array.shape[1:])


def per_device(
    features,
    coords,
    near_pairs,
    parent_two,
    parent_three,
    rates,
    w_near,
    restrict,
    w_two,
    w_three,
    w_four,
    coupling,
    expand,
    w_out,
):
    dev_count = lax.axis_size("dev")
    dev_index = lax.axis_index("dev")
    group_index = lax.axis_index("group")
    points_n, channels = features.shape
    blk_points = expand.shape[0]
    summary_rows = expand.shape[1]
    block_count = points_n // blk_points
    head_count = rates.shape[0]
    block_range = jnp.arange(block_count, dtype=jnp.int32)
    values = jnp.dot(features, w_near, preferred_element_type=jnp.float32).astype(jnp.bfloat16)
    vblocks = values.reshape(block_count, blk_points, channels)
    cblocks = coords.reshape(3, block_count, blk_points).transpose(1, 0, 2)

    def self_term(operands):
        cloud, block_values = operands
        return apply_table(kernel_table(cloud, cloud, rates), block_values, head_count, False)

    near_field = lax.map(
        self_term,
        (cblocks.reshape(-1, 4, 3, blk_points), vblocks.reshape(-1, 4, blk_points, channels)),
    )
    near_field = near_field.reshape(block_count, blk_points * channels)
    first_block = near_pairs[0]
    second_block = near_pairs[1]
    owner_first = first_block // block_count
    owner_second = second_block // block_count
    pair_key = owner_first * dev_count + owner_second
    position = jnp.arange(first_block.shape[0], dtype=jnp.int32)
    slot_rank = jnp.sum(
        (pair_key[:, None] == pair_key[None, :]) & (position[None, :] < position[:, None]), axis=1
    )
    slot_rows = dev_count * CAP
    row_range = jnp.arange(slot_rows, dtype=jnp.int32)
    peer_of_row = row_range // CAP
    slot_of_row = row_range % CAP
    same_slot = slot_rank[None, :] == slot_of_row[:, None]
    match_first = (
        (owner_first[None, :] == dev_index)
        & (owner_second[None, :] == peer_of_row[:, None])
        & same_slot
    )
    match_second = (
        (owner_first[None, :] == peer_of_row[:, None])
        & (owner_second[None, :] == dev_index)
        & same_slot
    )
    live_first = jnp.any(match_first, axis=1)
    live_second = jnp.any(match_second, axis=1)
    index_first = jnp.sum(jnp.where(match_first, first_block[None, :] % block_count, 0), axis=1)
    index_second = jnp.sum(jnp.where(match_second, second_block[None, :] % block_count, 0), axis=1)
    weight = live_second.astype(jnp.bfloat16)
    picked_values = (vblocks[index_second] * weight[:, None, None]).reshape(
        dev_count, CAP, blk_points, channels
    )
    picked_coords = (cblocks[index_second] * weight[:, None, None]).reshape(
        dev_count, CAP, 3, blk_points
    )
    mine_values = vblocks[index_first]
    mine_coords = cblocks[index_first]
    onehot_second = ((index_second[None, :] == block_range[:, None]) & live_second[None, :]).astype(
        jnp.bfloat16
    )

    def accumulate(running, side, index, live_rows):
        flat_side = side.reshape(side.shape[0], -1) * live_rows[:, None]
        return running.at[index].add(flat_side)

    got_values, got_coords = (
        lax.all_to_all(picked_values, "dev", split_axis=0, concat_axis=0, tiled=True),
        lax.all_to_all(picked_coords, "dev", split_axis=0, concat_axis=0, tiled=True),
    )
    got_values = got_values.reshape(slot_rows, blk_points, channels)
    got_coords = got_coords.reshape(slot_rows, 3, blk_points)

    def pair_step(running, operands):
        first_pos, second_pos, first_vals, second_vals, index, live_rows = operands
        kernel = kernel_table(first_pos, second_pos, rates)
        side_first = apply_table(kernel, second_vals, head_count, False)
        side_second = apply_table(kernel, first_vals, head_count, True) * live_rows[:, None, None]
        return (accumulate(running, side_first, index, live_rows), side_second.astype(jnp.bfloat16))

    near_field, side_second = lax.scan(
        pair_step,
        near_field,
        (
            in_groups(mine_coords),
            in_groups(got_coords),
            in_groups(mine_values),
            in_groups(got_values),
            in_groups(index_first),
            in_groups(live_first.astype(jnp.float32)),
        ),
    )
    returned = lax.all_to_all(
        side_second.reshape(dev_count, CAP, blk_points, channels),
        "dev",
        split_axis=0,
        concat_axis=0,
        tiled=True,
    )
    near_field = near_field + jnp.dot(
        onehot_second, returned.reshape(slot_rows, -1), preferred_element_type=jnp.float32
    )
    level_one = jnp.einsum(
        "sb,nbc->nsc",
        restrict,
        features.reshape(block_count, blk_points, channels),
        preferred_element_type=jnp.float32,
    )
    level_one = level_one.astype(jnp.bfloat16).reshape(block_count, summary_rows * channels)
    nodes_group = parent_three.shape[0]
    coarse_range = jnp.arange(NODES3_GROUP, dtype=jnp.int32)
    coarse_scale = NODES3_GROUP / nodes_group
    select_all = (parent_two[None, :] == jnp.arange(nodes_group, dtype=jnp.int32)[:, None]).astype(
        jnp.bfloat16
    )
    partial_two = jnp.dot(select_all, level_one, preferred_element_type=jnp.float32)
    flat = lax.psum(partial_two, "dev").astype(jnp.bfloat16).reshape(-1, channels)
    result = jax.nn.gelu(jnp.dot(flat, w_two, preferred_element_type=jnp.float32)).astype(
        jnp.bfloat16
    )
    level_two = result.reshape(-1, summary_rows * channels)
    select = (parent_three[None, :] == coarse_range[:, None]).astype(jnp.bfloat16)
    level_three = jnp.dot(select, level_two, preferred_element_type=jnp.float32)
    level_three = (level_three * coarse_scale).astype(jnp.bfloat16)
    three_all = lax.all_gather(level_three, "group", axis=0, tiled=True)
    coupling_rows = lax.dynamic_slice_in_dim(coupling, group_index * NODES3_GROUP, NODES3_GROUP, 0)
    mixed_three = jnp.dot(coupling_rows, three_all, preferred_element_type=jnp.float32).astype(
        jnp.bfloat16
    )
    down_three = jax.nn.gelu(
        jnp.dot(mixed_three.reshape(-1, channels), w_three, preferred_element_type=jnp.float32)
    )
    down_three = down_three.astype(jnp.bfloat16).reshape(NODES3_GROUP, summary_rows * channels)
    lift_table = (parent_three[:, None] == coarse_range[None, :]).astype(jnp.bfloat16)
    lifted = jnp.dot(
        level_two.reshape(-1, channels), w_four, preferred_element_type=jnp.float32
    ).reshape(-1, summary_rows * channels)
    down_two = jax.nn.gelu(
        lifted + jnp.dot(lift_table, down_three, preferred_element_type=jnp.float32)
    ).astype(jnp.bfloat16)
    select_parent = (
        parent_two[:, None] == jnp.arange(nodes_group, dtype=jnp.int32)[None, :]
    ).astype(jnp.bfloat16)
    parent_down = jnp.dot(select_parent, down_two, preferred_element_type=jnp.float32).astype(
        jnp.bfloat16
    )
    far_field = jnp.einsum(
        "bs,nsc->nbc",
        expand,
        parent_down.reshape(block_count, summary_rows, channels),
        preferred_element_type=jnp.float32,
    )
    far_field = far_field.astype(jnp.bfloat16).reshape(points_n, channels)
    total = near_field.reshape(points_n, channels) * blk_points ** (-0.5) + jnp.dot(
        far_field, w_out, preferred_element_type=jnp.float32
    )
    return total.astype(jnp.bfloat16)


def solution(mesh):
    placed = (
        P(("group", "dev"), None),
        P(None, ("group", "dev")),
        P(None, "group"),
        P(("group", "dev")),
        P("group"),
        P(),
        P(),
        P(),
        P(),
        P(),
        P(),
        P(),
        P(),
        P(),
    )
    return jax.shard_map(
        per_device, mesh=mesh, in_specs=placed, out_specs=P(("group", "dev"), None), check_vma=False
    )
```

profile of v0, /device:TPU:0, one launch (start us, length us, event | category | flops | bytes accessed | tf_op | source)
XLA Modules:
  0.0 172.9 jit_solution(7993352973277343777)
XLA Ops:
  0.0 0.8 fusion.100
  0.8 0.8 compare_bitcast_fusion.1
  2.3 1.4 gather_fusion.1
  3.6 0.7 copy_multiply_fusion
  4.3 7.3 %all-to-all-start = ((bf16[8,2,3,256]{3,1,2,0:T(2,128)(2,1)}), bf16[8,2,3,256]{3,1,2,0:T(2,128)(2,1)S(1)}, u32[]{:S(2)}, u32[]{:S(2)}) async-start(bf16[8,2,3,256]{3,1,2,0:T(2,128)(2,1)} %copy_multiply_fusion), calls=%async_computation | async-start | bytes 49152 | tf_op jit(solution)/shard_map/all_to_all | solution.py:120
  11.6 1.2 convolution_convert_fusion.2
  12.9 0.7 gather_fusion.2
  13.6 1.1 broadcast_multiply_fusion
  14.8 3.5 %all-to-all-done = bf16[8,2,3,256]{3,1,2,0:T(2,128)(2,1)S(1)} async-done(((bf16[8,2,3,256]{3,1,2,0:T(2,128)(2,1)}), bf16[8,2,3,256]{3,1,2,0:T(2,128)(2,1)S(1)}, u32[]{:S(2)}, u32[]{:S(2)}) %all-to-all-start) | async-done | bytes 24608 | tf_op jit(solution)/shard_map/all_to_all | solution.py:120
  18.3 4.2 %all-to-all-start.1 = ((bf16[8,2,256,128]{3,2,1,0:T(8,128)(2,1)}), bf16[8,2,256,128]{3,2,1,0:T(8,128)(2,1)}, u32[]{:S(2)}, u32[]{:S(2)}) async-start(bf16[8,2,256,128]{3,2,1,0:T(8,128)(2,1)} %broadcast_multiply_fusion), calls=%async_computation.1 | async-start | bytes 2097152 | tf_op jit(solution)/shard_map/all_to_all | solution.py:119
  22.5 8.8 %while.26 = (s32[]{:T(128)}, f32[4,4,256,128]{3,2,1,0:T(8,128)}, f32[1,4,1,1]{1,3,2,0:T(1,128)S(1)}, bf16[4,4,3,256]{3,1,2,0:T(4,128)(2,1)S(1)}, bf16[4,4,256,128]{3,2,1,0:T(8,128)(2,1)S(1)}, /*index=5*/s32[]{:T(128)}) while((s32[]{:T(128)}, f32[4,4,256,128]{3,2,1,0:T(8,128)}, f32[1,4,1,1]{1,3,2,0:T(1,128)S(1)}, ...), condition=%wide.region_1.2_spmd, body=%wide.region_0.1_spmd.sunk | while | flops 273159168 | bytes 3466345 | solution.py:68
  22.6 0.5 multiply_add_fusion.4
  23.1 1.6 fusion.134
  25.3 1.6 fusion.134
  27.5 1.7 fusion.134
  29.7 1.6 fusion.134
  31.4 0.6 gather_fusion
  32.0 1.7 gather_fusion.3
  34.3 74.6 %all-reduce.1 = bf16[32,8192]{1,0:T(8,128)(2,1)S(1)} all-reduce(f32[32,8192]{1,0:T(8,128)S(1)} %fusion.78), channel_id=1, replica_groups=mesh['group'=4,'dev'=8] {'dev'}, use_global_device_ids=true, to_apply=%region_10.11 | all-reduce | flops 262144 | bytes 1572864 | tf_op jit(solution)/shard_map/psum | solution.py:168
  109.0 1.1 reshape.359
  110.0 2.8 %copy.67 = f32[2,8,256,128]{3,1,2,0:T(8,128)S(1)} copy(f32[2,8,256,128]{3,2,1,0:T(8,128)} %bitcast.216) | data formatting | bytes 4194304
  112.9 22.6 %while.27 = (s32[]{:T(128)}, f32[16,32768]{1,0:T(8,128)S(1)}, bf16[2,8,256,128]{3,2,1,0:T(8,128)(2,1)}, s32[2,8]{1,0:T(2,128)S(1)}, f32[1,4,1,1]{1,3,2,0:T(1,128...) while((s32[]{:T(128)}, f32[16,32768]{1,0:T(8,128)S(1)}, ...), condition=%wide.region_9.10_spmd, body=%wide.region_7.9_spmd.sunk | while | flops 1089484800 | bytes 16478605 | solution.py:132
  113.0 1.3 dynamic-slice_bitcast_fusion.6
  114.3 0.9 multiply_add_fusion.5
  115.2 2.3 %fusion.141 = bf16[2,8,256,128]{3,2,1,0:T(8,128)(2,1)} fusion(bf16[2,8,256,128]{3,2,1,0:T(8,128)(2,1)} %get-tuple-element.456, s32[]{:T(128)S(6)} %copy.82, f32[8,256,256]{1,2,0:T(8,128)S(1)} %multiply_add_fusion.5, f32[4]{0:T(128)S(1)} %bitcast.229, bf16[8,256,128]{2,1,0:T(8,128)(2,1)S(1)} %get-tuple-element.424, bf16[4,128]{1,0:T(4,128)(2,1)S(1)} %fusion.138, ...), kind=kOutput, calls=%fused_computation.41.clone.1 | convolution fusion | flops 542638080 | bytes 3146804 | tf_op jit(solution)/shard_map/while/body/eval_jaxpr/nhqp,nhqc->npc/dot_general | solution.py:28
  117.5 1.9 %fusion.139 = f32[1,8,256,128]{3,2,1,0:T(8,128)S(1)} fusion(f32[8,256,256]{1,2,0:T(8,128)S(1)} %multiply_add_fusion.5, f32[4]{0:T(128)S(1)} %bitcast.230, bf16[4,128]{1,0:T(4,128)(2,1)S(1)} %fusion.138, bf16[8,256,128]{2,1,0:T(8,128)(2,1)S(1)} %get-tuple-element.423), kind=kOutput, calls=%fused_computation.36.clone.1 | convolution fusion | flops 542113792 | bytes 3671056 | tf_op jit(solution)/shard_map/while/body/eval_jaxpr/nhpq,nhqc->npc/dot_general | solution.py:28
  119.4 1.6 bitcast_multiply_fusion.2
  121.0 3.2 %scatter_fusion = f32[16,32768]{1,0:T(8,128)S(1)} fusion(f32[16,32768]{1,0:T(8,128)S(1)} %get-tuple-element.455, s32[8]{0:T(128)S(1)} %fusion.137, f32[8,32768]{1,0:T(8,128)} %bitcast_multiply_fusion.2), kind=kCustom, calls=%fused_computation.4.clone.1 | custom fusion | flops 262144 | bytes 3145760 | tf_op jit(solution)/shard_map/while/body/eval_jaxpr/scatter-add | solution.py:116
  124.3 1.3 dynamic-slice_bitcast_fusion.6
  125.6 0.9 multiply_add_fusion.5
  126.5 2.3 %fusion.141 = bf16[2,8,256,128]{3,2,1,0:T(8,128)(2,1)} fusion(bf16[2,8,256,128]{3,2,1,0:T(8,128)(2,1)} %get-tuple-element.456, s32[]{:T(128)S(6)} %copy.82, f32[8,256,256]{1,2,0:T(8,128)S(1)} %multiply_add_fusion.5, f32[4]{0:T(128)S(1)} %bitcast.229, bf16[8,256,128]{2,1,0:T(8,128)(2,1)S(1)} %get-tuple-element.424, bf16[4,128]{1,0:T(4,128)(2,1)S(1)} %fusion.138, ...), kind=kOutput, calls=%fused_computation.41.clone.1 | convolution fusion | flops 542638080 | bytes 3146804 | tf_op jit(solution)/shard_map/while/body/eval_jaxpr/nhqp,nhqc->npc/dot_general | solution.py:28
  128.8 1.9 %fusion.139 = f32[1,8,256,128]{3,2,1,0:T(8,128)S(1)} fusion(f32[8,256,256]{1,2,0:T(8,128)S(1)} %multiply_add_fusion.5, f32[4]{0:T(128)S(1)} %bitcast.230, bf16[4,128]{1,0:T(4,128)(2,1)S(1)} %fusion.138, bf16[8,256,128]{2,1,0:T(8,128)(2,1)S(1)} %get-tuple-element.423), kind=kOutput, calls=%fused_computation.36.clone.1 | convolution fusion | flops 542113792 | bytes 3671056 | tf_op jit(solution)/shard_map/while/body/eval_jaxpr/nhpq,nhqc->npc/dot_general | solution.py:28
  130.7 1.6 bitcast_multiply_fusion.2
  132.3 3.2 %scatter_fusion = f32[16,32768]{1,0:T(8,128)S(1)} fusion(f32[16,32768]{1,0:T(8,128)S(1)} %get-tuple-element.455, s32[8]{0:T(128)S(1)} %fusion.137, f32[8,32768]{1,0:T(8,128)} %bitcast_multiply_fusion.2), kind=kCustom, calls=%fused_computation.4.clone.1 | custom fusion | flops 262144 | bytes 3145760 | tf_op jit(solution)/shard_map/while/body/eval_jaxpr/scatter-add | solution.py:116
  135.5 4.4 %all-to-all-start.2 = ((bf16[8,2,256,128]{3,2,1,0:T(8,128)(2,1)}), bf16[8,2,256,128]{3,2,1,0:T(8,128)(2,1)}, u32[]{:S(2)}, u32[]{:S(2)}) async-start(bf16[8,2,256,128]{3,2,1,0:T(8,128)(2,1)} %bitcast.56), calls=%async_computation.2 | async-start | bytes 2097152 | tf_op jit(solution)/shard_map/all_to_all | solution.py:144
  140.0 2.4 %fusion.55 = bf16[2048,128]{1,0:T(8,128)(2,1)} fusion(bf16[2048,128]{1,0:T(8,128)(2,1)} %reshape.359, bf16[128,128]{1,0:T(8,128)(2,1)S(1)} %copy-done.6), kind=kOutput, calls=%fused_computation.93 | convolution fusion | flops 69468160 | bytes 1081344 | tf_op jit(solution)/shard_map/dot_general | solution.py:169
  142.4 2.1 %reshape.361 = bf16[32,8192]{1,0:T(8,128)(2,1)} reshape(bf16[2048,128]{1,0:T(8,128)(2,1)} %fusion.55) | data formatting | bytes 1048576 | tf_op jit(solution)/shard_map/reshape | solution.py:172
  144.4 1.2 fusion.44
  145.6 7.2 %all_gather.3 = bf16[32,8192]{1,0:T(8,128)(2,1)S(1)} all-gather(bf16[8,8192]{1,0:T(8,128)(2,1)S(1)} %fusion.44), channel_id=1, replica_groups=mesh['group'=4,'dev'=8] {'group'}, dimensions={0}, use_global_device_ids=true | all-gather | bytes 655360 | tf_op jit(solution)/shard_map/all_gather | solution.py:176
  152.8 0.9 convolution_convert_fusion.1
  154.1 2.3 %fusion.106 = f32[2048,128]{1,0:T(8,128)} fusion(bf16[2048,128]{1,0:T(8,128)(2,1)} %fusion.55, bf16[128,128]{1,0:T(8,128)(2,1)} %param.28), kind=kOutput, calls=%fused_computation.189 | convolution fusion | flops 67108864 | bytes 1605632 | tf_op jit(solution)/shard_map/dot_general | solution.py:186
  156.4 2.4 %reshape.360 = f32[32,8192]{1,0:T(8,128)} reshape(f32[2048,128]{1,0:T(8,128)} %fusion.106) | data formatting | bytes 2097152 | tf_op jit(solution)/shard_map/reshape | solution.py:188
  158.8 1.9 %fusion.47 = bf16[2,8,64,128]{3,1,2,0:T(8,128)(2,1)S(1)} fusion(f32[32,8192]{1,0:T(8,128)} %reshape.360, bf16[8,8192]{1,0:T(8,128)(2,1)S(1)} %reshape.363, s32[32]{0:T(128)S(1)} %copy-done.5, s32[16]{0:T(128)S(1)} %copy-done.4), kind=kOutput, calls=%fused_computation.85 | convolution fusion | flops 15336192 | bytes 1441984 | tf_op jit(solution)/shard_map/dot_general | solution.py:195
  160.8 2.2 %fusion.46 = bf16[16,256,128]{1,2,0:T(8,128)(2,1)} fusion(bf16[16,64,128]{2,1,0:T(8,128)(2,1)S(1)} %bitcast.218, bf16[256,64]{0,1:T(8,128)(2,1)} %param.30), kind=kOutput, calls=%fused_computation.83 | convolution fusion | flops 67633152 | bytes 1343488 | tf_op jit(solution)/shard_map/bs,nsc->nbc/dot_general | solution.py:198
  162.9 2.3 %copy.41 = bf16[16,256,128]{2,1,0:T(8,128)(2,1)} copy(bf16[16,256,128]{1,2,0:T(8,128)(2,1)} %fusion.46) | data formatting | bytes 2097152 | tf_op jit(solution)/shard_map/convert_element_type | solution.py:204
  165.2 3.3 %fusion.43 = f32[16,32768]{1,0:T(8,128)} fusion(f32[16,32768]{1,0:T(8,128)S(1)} %get-tuple-element.203, bf16[2,8,256,128]{3,2,1,0:T(8,128)(2,1)} %bitcast.73, s32[16]{0:T(128)S(1)} %get-tuple-element.252, pred[16]{0:T(512)(128)(4,1)S(1)} %get-tuple-element.251), kind=kOutput, calls=%fused_computation.70 | convolution fusion | flops 17826304 | bytes 5242960 | tf_op jit(solution)/shard_map/dot_general | solution.py:151
  168.5 1.7 mul.354
  170.3 2.6 %fusion.45 = bf16[4096,128]{1,0:T(8,128)(2,1)} fusion(f32[4096,128]{1,0:T(8,128)S(1)} %mul.354, bf16[4096,128]{1,0:T(8,128)(2,1)} %bitcast.215, bf16[128,128]{1,0:T(8,128)(2,1)S(1)} %copy-done.2), kind=kOutput, calls=%fused_computation.77 | convolution fusion | flops 135266304 | bytes 4227072 | tf_op jit(solution)/shard_map/dot_general | solution.py:205
  (85 shorter events, 3.7 us)
Async XLA Ops:
  0.0 11.6 %copy-start = (bf16[4096,128]{1,0:T(8,128)(2,1)S(1)}, bf16[4096,128]{1,0:T(8,128)(2,1)}, u32[]{:S(2)}) copy-start(bf16[4096,128]{1,0:T(8,128)(2,1)} %param.18) | copy-start | bytes 3145732
  4.3 13.9 %all-to-all-start = ((bf16[8,2,3,256]{3,1,2,0:T(2,128)(2,1)}), bf16[8,2,3,256]{3,1,2,0:T(2,128)(2,1)S(1)}, u32[]{:S(2)}, u32[]{:S(2)}) async-start(bf16[8,2,3,256]{3,1,2,0:T(2,128)(2,1)} %copy_multiply_fusion), calls=%async_computation | async-start | bytes 49152 | tf_op jit(solution)/shard_map/all_to_all | solution.py:120
  12.8 1.9 %copy-start.8 = (f32[4]{0:T(128)S(1)}, f32[4]{0:T(128)}, u32[]{:S(2)}) copy-start(f32[4]{0:T(128)} %param.23) | copy-start | bytes 52
  12.8 1.9 %copy-start.1 = (bf16[3,4096]{1,0:T(4,128)(2,1)S(1)}, bf16[3,4096]{1,0:T(4,128)(2,1)}, u32[]{:S(2)}) copy-start(bf16[3,4096]{1,0:T(4,128)(2,1)} %param.19) | copy-start | bytes 73732
  18.3 94.6 %all-to-all-start.1 = ((bf16[8,2,256,128]{3,2,1,0:T(8,128)(2,1)}), bf16[8,2,256,128]{3,2,1,0:T(8,128)(2,1)}, u32[]{:S(2)}, u32[]{:S(2)}) async-start(bf16[8,2,256,128]{3,2,1,0:T(8,128)(2,1)} %broadcast_multiply_fusion), calls=%async_computation.1 | async-start | bytes 2097152 | tf_op jit(solution)/shard_map/all_to_all | solution.py:119
  31.3 2.5 %copy-start.3 = (bf16[64,256]{1,0:T(8,128)(2,1)S(1)}, bf16[64,256]{1,0:T(8,128)(2,1)}, u32[]{:S(2)}) copy-start(bf16[64,256]{1,0:T(8,128)(2,1)} %param.25) | copy-start | bytes 98308
  31.3 2.8 %copy-start.4 = (s32[16]{0:T(128)S(1)}, s32[16]{0:T(128)}, u32[]{:S(2)}) copy-start(s32[16]{0:T(128)} %param.21) | copy-start | bytes 196
  135.5 4.5 %copy-start.6 = (bf16[128,128]{1,0:T(8,128)(2,1)S(1)}, bf16[128,128]{1,0:T(8,128)(2,1)}, u32[]{:S(2)}) copy-start(bf16[128,128]{1,0:T(8,128)(2,1)} %param.26) | copy-start | bytes 98308
  135.5 29.7 %all-to-all-start.2 = ((bf16[8,2,256,128]{3,2,1,0:T(8,128)(2,1)}), bf16[8,2,256,128]{3,2,1,0:T(8,128)(2,1)}, u32[]{:S(2)}, u32[]{:S(2)}) async-start(bf16[8,2,256,128]{3,2,1,0:T(8,128)(2,1)} %bitcast.56), calls=%async_computation.2 | async-start | bytes 2097152 | tf_op jit(solution)/shard_map/all_to_all | solution.py:144
  140.0 4.4 %copy-start.5 = (s32[32]{0:T(128)S(1)}, s32[32]{0:T(128)}, u32[]{:S(2)}) copy-start(s32[32]{0:T(128)} %param.22) | copy-start | bytes 388
  142.4 11.4 %copy-start.7 = (bf16[128,128]{1,0:T(8,128)(2,1)S(1)}, bf16[128,128]{1,0:T(8,128)(2,1)}, u32[]{:S(2)}) copy-start(bf16[128,128]{1,0:T(8,128)(2,1)} %param.27) | copy-start | bytes 98308
  168.5 1.7 %copy-start.2 = (bf16[128,128]{1,0:T(8,128)(2,1)S(1)}, bf16[128,128]{1,0:T(8,128)(2,1)}, u32[]{:S(2)}) copy-start(bf16[128,128]{1,0:T(8,128)(2,1)} %param.31) | copy-start | bytes 98308
where the time goes:
time: 174 us; the launch traced here: 173 us
  blocking collectives  81.8 us (47%)
  matrix products  33.8 us (19%)
  local copies, waits for them, and re-layouts  19.9 us (11%)
  other arithmetic  17.3 us (10%)
  starting transfers between devices  16 us (9%)
  waiting for transfers between devices  3.51 us (2%)
    psum x1, blocking collectives, per_device(): lax.psum(partial_two, 'dev').astype(jnp.bfloat16).reshape(-1, channels)  74.6 us
    dot_general x8, matrix products, apply_table(): return jnp.einsum(form, kernel, masked, preferred_element_type=jnp.float32)  15 us
    all_to_all x1, starting transfers between devices, per_device(): lax.all_to_all(picked_coords, 'dev', split_axis=0, concat_axis=0, tiled=T...  7.31 us
    all_gather x1, blocking collectives, per_device(): three_all = lax.all_gather(level_three, 'group', axis=0, tiled=True)  7.18 us
    scatter-add x2, other arithmetic, accumulate(): return running.at[index].add(flat_side)  6.32 us
    all_to_all x1, starting transfers between devices, per_device(): lax.all_to_all(side_second.reshape(dev_count, CAP, blk_points, channels),...  4.44 us
    all_to_all x1, starting transfers between devices, per_device(): lax.all_to_all(picked_values, 'dev', split_axis=0, concat_axis=0, tiled=T...  4.25 us
    add x6, other arithmetic, kernel_table(): distance = delta_x * delta_x + delta_y * delta_y + delta_z * delta_z  3.65 us
  transfers between devices with their start and end apart: 3, of which 1 were waited for; matrix products, arithmetic and copies ran while one was open for 21% of the time, Pallas kernels for 0%

commit v1 on v0

v1 whole, which is shorter than its diff:
```python
import functools
import math

import jax
import jax.numpy as jnp
from jax import lax
from jax.experimental import pallas as pl
from jax.experimental.pallas import tpu as pltpu
from jax.sharding import PartitionSpec as P

CAP = 2
SLOTS = 2 * CAP
AUG = 16
ROWS = 8
LOG2E = math.log2(math.e)
MESH = pl.DeviceIdType.MESH
F32 = jnp.float32
BF16 = jnp.bfloat16


def mm(a, b):
    return jnp.dot(a, b, preferred_element_type=F32)


def iota(shape, axis):
    return lax.broadcasted_iota(jnp.int32, shape, axis)


def prepare(
    n_dev,
    pairs_ref,
    feat_ref,
    coords_ref,
    par_ref,
    wnear_ref,
    restrict_ref,
    vals_ref,
    pos_p_ref,
    pos_q_ref,
    send_v_ref,
    send_q_ref,
    pick_p_ref,
    partial_ref,
    index_ref,
    count_ref,
    level_ref,
):
    me = lax.axis_index("dev")
    blocks, points, channels = vals_ref.shape
    pairs_n = pairs_ref.shape[1]
    s_rows, nodes, _ = partial_ref.shape

    def clear(i, _):
        index_ref[i] = -1
        return 0

    lax.fori_loop(0, n_dev * SLOTS, clear, 0)

    def clear_count(i, _):
        count_ref[i] = 0
        return 0

    lax.fori_loop(0, n_dev * 2, clear_count, 0)

    def one_pair(k, _):
        a = pairs_ref[0, k]
        b = pairs_ref[1, k]
        own_a = a // blocks
        own_b = b // blocks

        @pl.when(own_a == me)
        def _():
            rank = count_ref[own_b]
            index_ref[own_b * SLOTS + rank] = a % blocks
            count_ref[own_b] = rank + 1

        @pl.when(own_b == me)
        def _():
            rank = count_ref[n_dev + own_a]
            index_ref[own_a * SLOTS + CAP + rank] = b % blocks
            count_ref[n_dev + own_a] = rank + 1

        return 0

    lax.fori_loop(0, pairs_n, one_pair, 0)

    xyz = coords_ref[...].astype(F32)
    norm = jnp.sum(xyz * xyz, axis=0, keepdims=True)
    one = norm.astype(BF16).astype(F32)
    two = (norm - one).astype(BF16).astype(F32)
    three = norm - one - two
    ones = jnp.ones_like(norm)
    pad = jnp.zeros((AUG - 9, norm.shape[1]), F32)
    aug_p = jnp.concatenate([-2.0 * xyz, one, two, three, ones, ones, ones, pad], axis=0).astype(BF16)
    aug_q = jnp.concatenate([xyz, ones, ones, ones, one, two, three, pad], axis=0).astype(BF16)
    for j in range(blocks):
        pos_p_ref[j] = aug_p[:, j * points : (j + 1) * points]
        pos_q_ref[j] = aug_q[:, j * points : (j + 1) * points]
        block = feat_ref[pl.ds(j * points, points), :]
        vals_ref[j] = mm(block, wnear_ref[...]).astype(BF16)
        level_ref[j] = mm(restrict_ref[...], block).astype(BF16).astype(F32)

    rows, cols = ROWS * nodes, blocks * ROWS
    row, col = iota((rows, cols), 0), iota((rows, cols), 1)
    spread = ((row // nodes == col % ROWS) & (row % nodes == par_ref[...])).astype(F32).astype(BF16)
    for c in range(s_rows // ROWS):
        part = level_ref[:, c * ROWS : (c + 1) * ROWS, :].reshape(cols, channels).astype(BF16)
        partial_ref[c * ROWS : (c + 1) * ROWS] = (
            mm(spread, part).astype(BF16).reshape(ROWS, nodes, channels)
        )

    def pick(i, _):
        local = jnp.maximum(index_ref[i], 0)
        to = (i // SLOTS) * SLOTS + (i + CAP) % SLOTS
        send_v_ref[to] = vals_ref[local]
        send_q_ref[to] = pos_q_ref[local]
        pick_p_ref[i] = pos_p_ref[local]
        return 0

    lax.fori_loop(0, n_dev * SLOTS, pick, 0)


def table_apply(pos_p, pos_q, values, rates_ref, heads):
    d2 = lax.dot_general(pos_p, pos_q, (((0,), (0,)), ((), ())), preferred_element_type=F32)
    channels = values.shape[1]
    head_of = iota(values.shape, 1) // (channels // heads)
    total = None
    for h in range(heads):
        kernel = jnp.exp2((d2 * (rates_ref[h] * (-LOG2E))).astype(BF16))
        term = mm(kernel, jnp.where(head_of == h, values, jnp.zeros_like(values)))
        total = term if total is None else total + term
    return total


def exchange(
    n_dev,
    n_group,
    rates_ref,
    vals_ref,
    pos_p_ref,
    pos_q_ref,
    pick_p_ref,
    send_v_ref,
    send_q_ref,
    partial_ref,
    p3_lane_ref,
    p3_col_ref,
    wtwo_ref,
    wthree_ref,
    wfour_ref,
    coupling_ref,
    self_ref,
    side_ref,
    down_ref,
    got_v,
    got_q,
    got_part,
    got_three,
    got_down,
    three_buf,
    down_buf,
    v_sems,
    q_sems,
    part_sems,
    three_sems,
    down_sems,
    local_sems,
):
    me = lax.axis_index("dev")
    mine = lax.axis_index("group")
    heads = rates_ref.shape[0]
    blocks = vals_ref.shape[0]
    channels = vals_ref.shape[2]
    slice_rows, nodes, _ = got_part.shape[1:]
    nodes3 = coupling_ref.shape[0] // n_group

    def ahead(k):
        return (me + k) % n_dev

    barrier = pltpu.get_barrier_semaphore()

    def greet(k, _):
        pl.semaphore_signal(barrier, inc=1, device_id={"dev": ahead(k)}, device_id_type=MESH)
        return 0

    def greet_group(k, _):
        pl.semaphore_signal(barrier, inc=1, device_id={"group": (mine + k) % n_group}, device_id_type=MESH)
        return 0

    lax.fori_loop(1, n_dev, greet, 0)
    lax.fori_loop(1, n_group, greet_group, 0)

    def own_copies():
        return (
            pltpu.make_async_copy(partial_ref.at[pl.ds(me * slice_rows, slice_rows)], got_part.at[me], local_sems.at[0]),
            pltpu.make_async_copy(send_v_ref.at[me], got_v.at[me], local_sems.at[1]),
            pltpu.make_async_copy(send_q_ref.at[me], got_q.at[me], local_sems.at[2]),
        )

    for copy in own_copies():
        copy.start()
    pl.semaphore_wait(barrier, n_dev - 1 + n_group - 1)

    def dev_copy(src, dst, sems, k):
        return pltpu.make_async_remote_copy(
            src_ref=src,
            dst_ref=dst,
            send_sem=sems.at[0, k],
            recv_sem=sems.at[1, k],
            device_id={"dev": ahead(k)},
            device_id_type=MESH,
        )

    def part_copy(k):
        return dev_copy(
            partial_ref.at[pl.ds(ahead(k) * slice_rows, slice_rows)], got_part.at[me], part_sems, k
        )

    def v_copy(k):
        return dev_copy(send_v_ref.at[ahead(k)], got_v.at[me], v_sems, k)

    def q_copy(k):
        return dev_copy(send_q_ref.at[ahead(k)], got_q.at[me], q_sems, k)

    def down_copy(k):
        return dev_copy(down_buf, got_down.at[me], down_sems, k)

    def three_copy(k):
        return pltpu.make_async_remote_copy(
            src_ref=three_buf,
            dst_ref=got_three.at[mine],
            send_sem=three_sems.at[0, k],
            recv_sem=three_sems.at[1, k],
            device_id={"group": (mine + k) % n_group},
            device_id_type=MESH,
        )

    def each(fn, count):
        def body(k, _):
            fn(k)
            return 0

        lax.fori_loop(1, count, body, 0)

    each(lambda k: part_copy(k).start(), n_dev)
    each(lambda k: (q_copy(k).start(), v_copy(k).start()), n_dev)

    def self_tables(low, high):
        def body(j, _):
            self_ref[j] = table_apply(pos_p_ref[j], pos_q_ref[j], vals_ref[j], rates_ref, heads)
            return 0

        lax.fori_loop(low, high, body, 0)

    quarter = blocks // 4
    self_tables(0, quarter)
    for copy in own_copies():
        copy.wait()
    each(lambda k: part_copy(k).wait(), n_dev)

    rows = slice_rows * nodes
    rows3 = slice_rows * nodes3
    total = got_part[0].astype(F32)
    for d in range(1, n_dev):
        total = total + got_part[d].astype(F32)
    flat = total.reshape(rows, channels).astype(BF16)
    two = jax.nn.gelu(mm(flat, wtwo_ref[...])).astype(BF16)
    row, col = iota((rows3, rows), 0), iota((rows3, rows), 1)
    select = ((row // nodes3 == col // nodes) & (row % nodes3 == p3_lane_ref[...])).astype(F32).astype(BF16)
    three_buf[...] = (mm(select, two) * (nodes3 / nodes)).astype(BF16)
    lifted = mm(two, wfour_ref[...])
    self_tables(quarter, quarter + 1)
    each(lambda k: three_copy(k).start(), n_group)
    got_three[mine] = three_buf[...]
    self_tables(quarter + 1, 2 * quarter + quarter // 2)

    all3 = coupling_ref.shape[0]
    row, col = iota((rows3, all3), 0), iota((rows3, all3), 1)
    left = mm((col == mine * nodes3 + row % nodes3).astype(F32).astype(BF16), coupling_ref[...]).astype(BF16)
    row, col = iota((all3, n_group * rows3), 0), iota((all3, n_group * rows3), 1)
    right = (row == (col // rows3) * nodes3 + col % nodes3).astype(F32).astype(BF16)
    row, col = iota((rows3, n_group * rows3), 0), iota((rows3, n_group * rows3), 1)
    wide = jnp.where(row // nodes3 == (col % rows3) // nodes3, mm(left, right), 0.0).astype(BF16)
    row, col = iota((rows, rows3), 0), iota((rows, rows3), 1)
    lift = ((row // nodes == col // nodes3) & (p3_col_ref[...] == col % nodes3)).astype(F32).astype(BF16)

    each(lambda k: three_copy(k).wait(), n_group)
    mixed = mm(wide, got_three[...].reshape(n_group * rows3, channels)).astype(BF16)
    down3 = jax.nn.gelu(mm(mixed, wthree_ref[...])).astype(BF16)
    down2 = jax.nn.gelu(lifted + mm(lift, down3)).astype(BF16).reshape(slice_rows, nodes, channels)
    down_buf[...] = down2
    got_down[me] = down2
    self_tables(2 * quarter + quarter // 2, 2 * quarter + quarter // 2 + 1)
    each(lambda k: down_copy(k).start(), n_dev)
    self_tables(2 * quarter + quarter // 2 + 1, blocks)

    def side_of(k, _):
        source = (me + n_dev - k) % n_dev

        @pl.when(k > 0)
        def _():
            q_copy(k).wait()
            v_copy(k).wait()

        def one(j, _):
            side_ref[source, j] = table_apply(
                pick_p_ref[source, j], got_q[source, j], got_v[source, j], rates_ref, heads
            ).astype(BF16)
            return 0

        lax.fori_loop(0, SLOTS, one, 0)
        return 0

    lax.fori_loop(0, n_dev, side_of, 0)
    each(lambda k: down_copy(k).wait(), n_dev)
    down_ref[...] = got_down[...]


def finish(slots_n, index_ref, self_ref, side_ref, down_ref, par_ref, expand_ref, wout_ref, out_ref, acc, parent_down):
    blocks, points, channels = self_ref.shape
    s_rows, nodes, _ = down_ref.shape
    rows, cols = blocks * ROWS, ROWS * nodes
    row, col = iota((rows, cols), 0), iota((rows, cols), 1)
    gather = ((row % ROWS == col // nodes) & (par_ref[...] == col % nodes)).astype(F32).astype(BF16)
    for c in range(s_rows // ROWS):
        part = down_ref[c * ROWS : (c + 1) * ROWS].reshape(cols, channels)
        parent_down[:, c * ROWS : (c + 1) * ROWS, :] = mm(gather, part).reshape(blocks, ROWS, channels)
    acc[...] = self_ref[...]

    def add(i, _):
        local = index_ref[i]

        @pl.when(local >= 0)
        def _():
            acc[local] += side_ref[i].astype(F32)

        return 0

    lax.fori_loop(0, slots_n, add, 0)
    for j in range(blocks):
        far = mm(expand_ref[...], parent_down[j].astype(BF16)).astype(BF16)
        total = acc[j] * (points ** (-0.5)) + mm(far, wout_ref[...])
        out_ref[j * points : (j + 1) * points, :] = total.astype(BF16)


VMEM = pl.BlockSpec(memory_space=pltpu.VMEM)
SMEM = pl.BlockSpec(memory_space=pltpu.SMEM)
ANY = pl.BlockSpec(memory_space=pl.ANY)


def per_device(
    n_dev,
    n_group,
    features,
    coords,
    near_pairs,
    parent_two,
    parent_three,
    rates,
    w_near,
    restrict,
    w_two,
    w_three,
    w_four,
    coupling,
    expand,
    w_out,
):
    points_n, channels = features.shape
    points, s_rows = expand.shape
    blocks = points_n // points
    nodes = parent_three.shape[0]
    slots_n = n_dev * SLOTS
    slice_rows = s_rows // n_dev
    nodes3 = coupling.shape[0] // n_group
    rows = slice_rows * nodes
    shape = jax.ShapeDtypeStruct
    par = jnp.repeat(parent_two, ROWS)
    p3 = jnp.tile(parent_three, slice_rows)
    vals, pos_p, pos_q, send_v, send_q, pick_p, partial, index = pl.pallas_call(
        functools.partial(prepare, n_dev),
        out_shape=(
            shape((blocks, points, channels), BF16),
            shape((blocks, AUG, points), BF16),
            shape((blocks, AUG, points), BF16),
            shape((slots_n, points, channels), BF16),
            shape((slots_n, AUG, points), BF16),
            shape((slots_n, AUG, points), BF16),
            shape((s_rows, nodes, channels), BF16),
            shape((slots_n,), jnp.int32),
        ),
        in_specs=[SMEM] + [VMEM] * 5,
        out_specs=(VMEM,) * 7 + (SMEM,),
        scratch_shapes=[
            pltpu.SMEM((2 * n_dev,), jnp.int32),
            pltpu.VMEM((blocks, s_rows, channels), F32),
        ],
        name="prepare",
    )(near_pairs, features, coords, par.reshape(1, -1), w_near, restrict)
    dma = pltpu.SemaphoreType.DMA
    own, side, down = pl.pallas_call(
        functools.partial(exchange, n_dev, n_group),
        out_shape=(
            shape((blocks, points, channels), F32),
            shape((n_dev, SLOTS, points, channels), BF16),
            shape((n_dev, slice_rows, nodes, channels), BF16),
        ),
        in_specs=[SMEM] + [VMEM] * 4 + [ANY] * 3 + [VMEM] * 6,
        out_specs=(VMEM,) * 3,
        scratch_shapes=[
            pltpu.VMEM((n_dev, SLOTS, points, channels), BF16),
            pltpu.VMEM((n_dev, SLOTS, AUG, points), BF16),
            pltpu.VMEM((n_dev, slice_rows, nodes, channels), BF16),
            pltpu.VMEM((n_group, slice_rows * nodes3, channels), BF16),
            pltpu.VMEM((n_dev, slice_rows, nodes, channels), BF16),
            pltpu.VMEM((slice_rows * nodes3, channels), BF16),
            pltpu.VMEM((slice_rows, nodes, channels), BF16),
            dma((2, n_dev)),
            dma((2, n_dev)),
            dma((2, n_dev)),
            dma((2, n_group)),
            dma((2, n_dev)),
            dma((3,)),
        ],
        compiler_params=pltpu.CompilerParams(
            collective_id=0, has_side_effects=True, vmem_limit_bytes=60 * 1024 * 1024
        ),
        name="exchange",
    )(
        rates,
        vals,
        pos_p,
        pos_q,
        pick_p.reshape(n_dev, SLOTS, AUG, points),
        send_v.reshape(n_dev, SLOTS, points, channels),
        send_q.reshape(n_dev, SLOTS, AUG, points),
        partial,
        p3.reshape(1, -1),
        p3.reshape(-1, 1),
        w_two,
        w_three,
        w_four,
        coupling,
    )
    return pl.pallas_call(
        functools.partial(finish, slots_n),
        out_shape=shape((points_n, channels), BF16),
        in_specs=[SMEM] + [VMEM] * 6,
        out_specs=VMEM,
        scratch_shapes=[
            pltpu.VMEM((blocks, points, channels), F32),
            pltpu.VMEM((blocks, s_rows, channels), F32),
        ],
        name="finish",
    )(
        index,
        own,
        side.reshape(slots_n, points, channels),
        down.reshape(s_rows, nodes, channels),
        par.reshape(-1, 1),
        expand,
        w_out,
    )


def solution(mesh):
    placed = (
        P(("group", "dev"), None),
        P(None, ("group", "dev")),
        P(None, "group"),
        P(("group", "dev")),
        P("group"),
    ) + (P(),) * 9
    return jax.shard_map(
        functools.partial(per_device, mesh.shape["dev"], mesh.shape["group"]),
        mesh=mesh,
        in_specs=placed,
        out_specs=P(("group", "dev"), None),
        check_vma=False,
    )
```

time: 174 us -> 101 us (0.58)
  the two profiles are of different devices: /device:TPU:0 before, /device:TPU:28 now
where the time goes in v1:
time: 101 us
  Pallas kernels  95.8 us (95%)
  local copies, waits for them, and re-layouts  4.83 us (5%)
    pallas_call x1, Pallas kernels, per_device(): pl.pallas_call(functools.partial(exchange, n_dev, n_group), out_shape=(sh...  84.1 us
    pallas_call x1, Pallas kernels, per_device(): pl.pallas_call(functools.partial(prepare, n_dev), out_shape=(shape((block...  6.63 us
    pallas_call x1, Pallas kernels, per_device(): pl.pallas_call(functools.partial(finish, slots_n), out_shape=shape((point...  5.06 us

profile of v1, /device:TPU:28, one launch (start us, length us, event | category | flops | bytes accessed | tf_op | source)
XLA Modules:
  0.0 100.7 jit_solution(4542437154574279313)
XLA Ops:
  0.0 0.7 broadcast_in_dim.3
  0.7 0.6 reshape_reshape.6.par_ref
  1.3 6.6 %prepare.1 = (bf16[16,256,128]{2,1,0:T(8,128)(2,1)}, bf16[16,16,256]{2,1,0:T(8,128)(2,1)}, bf16[16,16,256]{2,1,0:T(8,128)(2,1)}, bf16[32,256,128]{2,1,0:T(8,128)...) custom-call(s32[2,64]{1,0:T(2,128)} %pairs_ref.1, ...), custom_call_target="tpu_custom_call" | custom-call | tf_op jit(solution)/shard_map/prepare/pallas_call | solution.py:380
  8.0 0.7 tile.2
  8.6 0.6 reshape_tile.6.p3_lane_ref
  9.2 0.8 reshape_tile.8.p3_col_ref
  10.0 0.0 copy-start
  10.0 84.1 %exchange.1 = (f32[16,256,128]{2,1,0:T(8,128)}, bf16[8,4,256,128]{3,2,1,0:T(8,128)(2,1)}, bf16[8,8,32,128]{3,2,1,0:T(8,128)(2,1)}) custom-call(f32[4]{0:T(128)} %rates_ref.1, bf16[16,256,128]{2,1,0:T(8,128)(2,1)} %get-tuple-element.17.vals_ref, bf16[16,16,256]{2,1,0:T(8,128)(2,1)} %get-tuple-element.18.pos_p_ref, ...), custom_call_target="tpu_custom_call" | custom-call | tf_op jit(solution)/shard_map/exchange/pallas_call | solution.py:401
  94.2 0.7 reshape_reshape.8.par_ref
  94.9 0.0 copy-done
  94.9 0.7 copy.19.expand_ref
  95.6 5.1 %finish.1 = bf16[4096,128]{1,0:T(8,128)(2,1)} custom-call(s32[32]{0:T(128)} %get-tuple-element.16.index_ref, f32[16,256,128]{2,1,0:T(8,128)} %get-tuple-element.24.self_ref, bf16[32,256,128]{2,1,0:T(8,128)(2,1)} %bitcast.5, bf16[64,32,128]{2,1,0:T(8,128)(2,1)} %bitcast.7, s32[128,1]{1,0:T(8,128)} %reshape_reshape.8.par_ref, ...), custom_call_target="tpu_custom_call" | custom-call | tf_op jit(solution)/shard_map/finish/pallas_call | solution.py:445
Async XLA Ops:
  10.0 84.8 %copy-start = (bf16[256,64]{0,1:T(8,128)(2,1)S(1)}, bf16[256,64]{0,1:T(8,128)(2,1)}, u32[]{:S(2)}) copy-start(bf16[256,64]{0,1:T(8,128)(2,1)} %param.26) | copy-start | bytes 98308

commit v2 on v1

--- a/solution.py
+++ b/solution.py
@@ -155,10 +155,10 @@
     got_v,
     got_q,
     got_part,
+    sum_part,
     got_three,
     got_down,
     three_buf,
-    down_buf,
     v_sems,
     q_sems,
     part_sems,
@@ -170,17 +170,24 @@
     mine = lax.axis_index("group")
     heads = rates_ref.shape[0]
     blocks = vals_ref.shape[0]
-    channels = vals_ref.shape[2]
-    slice_rows, nodes, _ = got_part.shape[1:]
+    s_rows, nodes, channels = partial_ref.shape
+    slice_rows = s_rows // n_dev
     nodes3 = coupling_ref.shape[0] // n_group
-
-    def ahead(k):
-        return (me + k) % n_dev
+    half_n = n_dev // 2
+    stages = n_dev.bit_length() - 1
+    bits = [(me // (1 << t)) % 2 for t in range(stages)]
+
+    def peer_of(mask):
+        other = 0
+        for t in range(stages):
+            flip = (mask // (1 << t)) % 2
+            other = other + (bits[t] + flip - 2 * bits[t] * flip) * (1 << t)
+        return other
 
     barrier = pltpu.get_barrier_semaphore()
 
     def greet(k, _):
-        pl.semaphore_signal(barrier, inc=1, device_id={"dev": ahead(k)}, device_id_type=MESH)
+        pl.semaphore_signal(barrier, inc=1, device_id={"dev": peer_of(k)}, device_id_type=MESH)
         return 0
 
     def greet_group(k, _):
@@ -192,38 +199,56 @@
 
     def own_copies():
         return (
-            pltpu.make_async_copy(partial_ref.at[pl.ds(me * slice_rows, slice_rows)], got_part.at[me], local_sems.at[0]),
-            pltpu.make_async_copy(send_v_ref.at[me], got_v.at[me], local_sems.at[1]),
-            pltpu.make_async_copy(send_q_ref.at[me], got_q.at[me], local_sems.at[2]),
+            pltpu.make_async_copy(send_v_ref.at[me], got_v.at[me], local_sems.at[0]),
+            pltpu.make_async_copy(send_q_ref.at[me], got_q.at[me], local_sems.at[1]),
         )
 
     for copy in own_copies():
         copy.start()
     pl.semaphore_wait(barrier, n_dev - 1 + n_group - 1)
 
-    def dev_copy(src, dst, sems, k):
+    def dev_copy(src, dst, sems, k, mask):
         return pltpu.make_async_remote_copy(
             src_ref=src,
             dst_ref=dst,
             send_sem=sems.at[0, k],
             recv_sem=sems.at[1, k],
-            device_id={"dev": ahead(k)},
+            device_id={"dev": peer_of(mask)},
             device_id_type=MESH,
         )
 
-    def part_copy(k):
+    upper = me // half_n
+    wide_rows = 2 * slice_rows
+    mine_rows = pl.ds((me % half_n) * wide_rows + upper * slice_rows, slice_rows)
+
+    def near_copy(mask):
+        src = partial_ref.at[pl.ds((peer_of(mask) % half_n) * wide_rows, wide_rows)]
+        return dev_copy(src, got_part.at[mask], part_sems, mask, mask)
+
+    def across_copy():
+        return dev_copy(sum_part.at[0], sum_part.at[1], part_sems, half_n, half_n)
+
+    def near_sum(side):
+        own = partial_ref[pl.ds((me % half_n) * wide_rows + side * slice_rows, slice_rows)].astype(F32)
+        for mask in range(1, half_n):
+            own = own + got_part[mask, pl.ds(side * slice_rows, slice_rows)].astype(F32)
+        return own
+
+    def down_across():
+        held = got_down.at[mine_rows]
+        return dev_copy(held, held, down_sems, half_n, half_n)
+
+    def down_near(mask):
+        held = got_down.at[pl.ds((me % half_n) * wide_rows, wide_rows)]
+        return dev_copy(held, held, down_sems, mask, mask)
+
+    def v_copy(mask, slot):
         return dev_copy(
-            partial_ref.at[pl.ds(ahead(k) * slice_rows, slice_rows)], got_part.at[me], part_sems, k
+            send_v_ref.at[peer_of(mask), slot], got_v.at[me, slot], v_sems, slot * n_dev + mask, mask
         )
 
-    def v_copy(k):
-        return dev_copy(send_v_ref.at[ahead(k)], got_v.at[me], v_sems, k)
-
-    def q_copy(k):
-        return dev_copy(send_q_ref.at[ahead(k)], got_q.at[me], q_sems, k)
-
-    def down_copy(k):
-        return dev_copy(down_buf, got_down.at[me], down_sems, k)
+    def q_copy(mask):
+        return dev_copy(send_q_ref.at[peer_of(mask)], got_q.at[me], q_sems, mask, mask)
 
     def three_copy(k):
         return pltpu.make_async_remote_copy(
@@ -235,44 +260,55 @@
             device_id_type=MESH,
         )
 
-    def each(fn, count):
+    def each(fn, low, high):
         def body(k, _):
             fn(k)
             return 0
 
-        lax.fori_loop(1, count, body, 0)
-
-    each(lambda k: part_copy(k).start(), n_dev)
-    each(lambda k: (q_copy(k).start(), v_copy(k).start()), n_dev)
-
-    def self_tables(low, high):
+        lax.fori_loop(low, high, body, 0)
+
+    def feed(slot):
+        each(lambda k: v_copy(k, slot).start(), half_n, n_dev)
+        each(lambda k: v_copy(k, slot).start(), 1, half_n)
+
+    done = [0]
+
+    def self_tables(count):
+        low, high = done[0], min(done[0] + count, blocks)
+        done[0] = high
+
         def body(j, _):
             self_ref[j] = table_apply(pos_p_ref[j], pos_q_ref[j], vals_ref[j], rates_ref, heads)
             return 0
 
-        lax.fori_loop(low, high, body, 0)
-
-    quarter = blocks // 4
-    self_tables(0, quarter)
-    for copy in own_copies():
-        copy.wait()
-    each(lambda k: part_copy(k).wait(), n_dev)
+        if high > low:
+            lax.fori_loop(low, high, body, 0)
+
+    each(lambda k: near_copy(k).start(), 1, half_n)
+    each(lambda k: q_copy(k).start(), 1, n_dev)
+    feed(0)
+    self_tables(4)
+    each(lambda k: near_copy(k).wait(), 1, half_n)
+    sum_part[0] = near_sum(1 - upper).astype(BF16)
+    self_tables(1)
+    across_copy().start()
+    feed(1)
+    own_sum = near_sum(upper)
+    self_tables(5)
+    across_copy().wait()
 
     rows = slice_rows * nodes
     rows3 = slice_rows * nodes3
-    total = got_part[0].astype(F32)
-    for d in range(1, n_dev):
-        total = total + got_part[d].astype(F32)
-    flat = total.reshape(rows, channels).astype(BF16)
+    flat = (own_sum + sum_part[1].astype(F32)).reshape(rows, channels).astype(BF16)
     two = jax.nn.gelu(mm(flat, wtwo_ref[...])).astype(BF16)
     row, col = iota((rows3, rows), 0), iota((rows3, rows), 1)
     select = ((row // nodes3 == col // nodes) & (row % nodes3 == p3_lane_ref[...])).astype(F32).astype(BF16)
     three_buf[...] = (mm(select, two) * (nodes3 / nodes)).astype(BF16)
     lifted = mm(two, wfour_ref[...])
-    self_tables(quarter, quarter + 1)
-    each(lambda k: three_copy(k).start(), n_group)
+    self_tables(1)
+    each(lambda k: three_copy(k).start(), 1, n_group)
     got_three[mine] = three_buf[...]
-    self_tables(quarter + 1, 2 * quarter + quarter // 2)
+    self_tables(1)
 
     all3 = coupling_ref.shape[0]
     row, col = iota((rows3, all3), 0), iota((rows3, all3), 1)
@@ -284,35 +320,41 @@
     row, col = iota((rows, rows3), 0), iota((rows, rows3), 1)
     lift = ((row // nodes == col // nodes3) & (p3_col_ref[...] == col % nodes3)).astype(F32).astype(BF16)
 
-    each(lambda k: three_copy(k).wait(), n_group)
+    each(lambda k: three_copy(k).wait(), 1, n_group)
     mixed = mm(wide, got_three[...].reshape(n_group * rows3, channels)).astype(BF16)
     down3 = jax.nn.gelu(mm(mixed, wthree_ref[...])).astype(BF16)
     down2 = jax.nn.gelu(lifted + mm(lift, down3)).astype(BF16).reshape(slice_rows, nodes, channels)
-    down_buf[...] = down2
-    got_down[me] = down2
-    self_tables(2 * quarter + quarter // 2, 2 * quarter + quarter // 2 + 1)
-    each(lambda k: down_copy(k).start(), n_dev)
-    self_tables(2 * quarter + quarter // 2 + 1, blocks)
-
-    def side_of(k, _):
-        source = (me + n_dev - k) % n_dev
-
-        @pl.when(k > 0)
-        def _():
-            q_copy(k).wait()
-            v_copy(k).wait()
-
-        def one(j, _):
-            side_ref[source, j] = table_apply(
-                pick_p_ref[source, j], got_q[source, j], got_v[source, j], rates_ref, heads
-            ).astype(BF16)
-            return 0
-
-        lax.fori_loop(0, SLOTS, one, 0)
-        return 0
-
-    lax.fori_loop(0, n_dev, side_of, 0)
-    each(lambda k: down_copy(k).wait(), n_dev)
+    got_down[mine_rows] = down2
+    self_tables(1)
+    down_across().start()
+    feed(2)
+    self_tables(blocks)
+    down_across().wait()
+    each(lambda k: down_near(k).start(), 1, half_n)
+    feed(3)
+    for copy in own_copies():
+        copy.wait()
+    each(lambda k: q_copy(k).wait(), 1, n_dev)
+
+    def side_table(mask, slot):
+        source = peer_of(mask)
+        side_ref[source, slot] = table_apply(
+            pick_p_ref[source, slot], got_q[source, slot], got_v[source, slot], rates_ref, heads
+        ).astype(BF16)
+
+    each(lambda j: side_table(0, j), 0, SLOTS)
+
+    def arrived(slot):
+        def body(k):
+            v_copy(k, slot).wait()
+            side_table(k, slot)
+
+        return body
+
+    for slot in range(SLOTS):
+        each(arrived(slot), half_n, n_dev)
+        each(arrived(slot), 1, half_n)
+    each(lambda k: down_near(k).wait(), 1, half_n)
     down_ref[...] = got_down[...]
 
 
@@ -373,7 +415,6 @@
     slots_n = n_dev * SLOTS
     slice_rows = s_rows // n_dev
     nodes3 = coupling.shape[0] // n_group
-    rows = slice_rows * nodes
     shape = jax.ShapeDtypeStruct
     par = jnp.repeat(parent_two, ROWS)
     p3 = jnp.tile(parent_three, slice_rows)
@@ -403,24 +444,24 @@
         out_shape=(
             shape((blocks, points, channels), F32),
             shape((n_dev, SLOTS, points, channels), BF16),
-            shape((n_dev, slice_rows, nodes, channels), BF16),
+            shape((s_rows, nodes, channels), BF16),
         ),
-        in_specs=[SMEM] + [VMEM] * 4 + [ANY] * 3 + [VMEM] * 6,
+        in_specs=[SMEM] + [VMEM] * 4 + [ANY] * 2 + [VMEM] * 7,
         out_specs=(VMEM,) * 3,
         scratch_shapes=[
             pltpu.VMEM((n_dev, SLOTS, points, channels), BF16),
             pltpu.VMEM((n_dev, SLOTS, AUG, points), BF16),
-            pltpu.VMEM((n_dev, slice_rows, nodes, channels), BF16),
+            pltpu.VMEM((n_dev // 2, 2 * slice_rows, nodes, channels), BF16),
+            pltpu.VMEM((2, slice_rows, nodes, channels), BF16),
             pltpu.VMEM((n_group, slice_rows * nodes3, channels), BF16),
-            pltpu.VMEM((n_dev, slice_rows, nodes, channels), BF16),
+            pltpu.VMEM((s_rows, nodes, channels), BF16),
             pltpu.VMEM((slice_rows * nodes3, channels), BF16),
-            pltpu.VMEM((slice_rows, nodes, channels), BF16),
-            dma((2, n_dev)),
+            dma((2, SLOTS * n_dev)),
             dma((2, n_dev)),
             dma((2, n_dev)),
             dma((2, n_group)),
             dma((2, n_dev)),
-            dma((3,)),
+            dma((2,)),
         ],
         compiler_params=pltpu.CompilerParams(
             collective_id=0, has_side_effects=True, vmem_limit_bytes=60 * 1024 * 1024
@@ -456,7 +497,7 @@
         index,
         own,
         side.reshape(slots_n, points, channels),
-        down.reshape(s_rows, nodes, channels),
+        down,
         par.reshape(-1, 1),
         expand,
         w_out,

time: 101 us -> 86.3 us (0.85)
  the two profiles are of different devices: /device:TPU:28 before, /device:TPU:0 now
where the time goes in v2:
time: 86.3 us; the launch traced here: 86.1 us
  Pallas kernels  81.3 us (94%)
  local copies, waits for them, and re-layouts  4.83 us (6%)
    pallas_call x1, Pallas kernels, per_device(): pl.pallas_call(functools.partial(exchange, n_dev, n_group), out_shape=(sh...  69.5 us
    pallas_call x1, Pallas kernels, per_device(): pl.pallas_call(functools.partial(prepare, n_dev), out_shape=(shape((block...  6.63 us
    pallas_call x1, Pallas kernels, per_device(): pl.pallas_call(functools.partial(finish, slots_n), out_shape=shape((point...  5.14 us

profile of v2, /device:TPU:0, one launch (start us, length us, event | category | flops | bytes accessed | tf_op | source)
XLA Modules:
  0.0 86.1 jit_solution(6671428775378009720)
XLA Ops:
  0.0 0.7 broadcast_in_dim.3
  0.7 0.6 reshape_reshape.6.par_ref
  1.3 6.6 %prepare.1 = (bf16[16,256,128]{2,1,0:T(8,128)(2,1)}, bf16[16,16,256]{2,1,0:T(8,128)(2,1)}, bf16[16,16,256]{2,1,0:T(8,128)(2,1)}, bf16[32,256,128]{2,1,0:T(8,128)...) custom-call(s32[2,64]{1,0:T(2,128)} %pairs_ref.1, ...), custom_call_target="tpu_custom_call" | custom-call | tf_op jit(solution)/shard_map/prepare/pallas_call | solution.py:421
  8.0 0.7 tile.2
  8.6 0.6 reshape_tile.6.p3_lane_ref
  9.2 0.8 reshape_tile.8.p3_col_ref
  10.0 0.0 copy-start
  10.0 69.5 %exchange.1 = (f32[16,256,128]{2,1,0:T(8,128)}, bf16[8,4,256,128]{3,2,1,0:T(8,128)(2,1)}, bf16[64,32,128]{2,1,0:T(8,128)(2,1)}) custom-call(f32[4]{0:T(128)} %rates_ref.1, bf16[16,256,128]{2,1,0:T(8,128)(2,1)} %get-tuple-element.17.vals_ref, bf16[16,16,256]{2,1,0:T(8,128)(2,1)} %get-tuple-element.18.pos_p_ref, ...), custom_call_target="tpu_custom_call" | custom-call | tf_op jit(solution)/shard_map/exchange/pallas_call | solution.py:442
  79.6 0.7 reshape_reshape.8.par_ref
  80.3 0.0 copy-done
  80.3 0.7 copy.19.expand_ref
  81.0 5.1 %finish.1 = bf16[4096,128]{1,0:T(8,128)(2,1)} custom-call(s32[32]{0:T(128)} %get-tuple-element.16.index_ref, f32[16,256,128]{2,1,0:T(8,128)} %get-tuple-element.24.self_ref, bf16[32,256,128]{2,1,0:T(8,128)(2,1)} %bitcast.4, bf16[64,32,128]{2,1,0:T(8,128)(2,1)} %get-tuple-element.26.down_ref, s32[128,1]{1,0:T(8,128)} %reshape_reshape.8.par_ref, ...), custom_call_target="tpu_custom_call" | custom-call | tf_op jit(solution)/shard_map/finish/pallas_call | solution.py:486
Async XLA Ops:
  10.0 70.2 %copy-start = (bf16[256,64]{0,1:T(8,128)(2,1)S(1)}, bf16[256,64]{0,1:T(8,128)(2,1)}, u32[]{:S(2)}) copy-start(bf16[256,64]{0,1:T(8,128)(2,1)} %param.26) | copy-start | bytes 98308
